TPU v7x, 32 devices: a whole 2x2x4 slice. The times are simulated.
32 devices in a mesh: shard: 4 (over z), tensor: 4 (over x, core), dp: 2 (over y).
Axes of the slice: x: 2, y: 2, z: 4, core: 2. Of those that a mesh axis runs over, the one named last changes fastest.
Arguments:
- gradient: bfloat16 [1, 8192, 8192], P(None, 'shard', ('tensor', 'dp')), may hold values from -16 to 16
- momentum: float32 [1, 8192, 8192], P(None, 'shard', ('tensor', 'dp')), may hold values from -16 to 16
- prior_right_factor: float32 [1, 8192, 128], P(None, ('tensor', 'dp')), may hold values from -8 to 8
Outputs:
- momentum_next: float32 [1, 8192, 8192], P(None, 'shard', ('tensor', 'dp'))
- following_right_factor: float32 [1, 8192, 128], P(None, ('tensor', 'dp'))
- direction: bfloat16 [1, 8192, 8192], P(None, 'shard', ('tensor', 'dp'))
All inputs are finite; a program needn't handle non-finite values.
Results may differ from a plain program's by a relative error of at most 0.0029.
Values sent between devices are 32-bit elements; how exact they have to be, the bound alone decides.
A program may use at most 64 MiB of HBM per device.

v0:
```python
import jax
import jax.numpy as jnp
from jax import lax
from jax.sharding import PartitionSpec as P

M = 8192
N = 8192
R = 128
decay_rate = 0.95
epsilon = 1e-06


def cholesky_pass(row_segment_block, summer):
    gram_matrix = summer(
        jnp.einsum(
            "ktp,ktv->kpv", row_segment_block, row_segment_block, precision=lax.Precision.HIGHEST
        )
    )
    factor_lower = jnp.linalg.cholesky(gram_matrix)
    return lax.linalg.triangular_solve(
        factor_lower, row_segment_block, left_side=False, lower=True, transpose_a=True
    )


def shards(gradient, momentum, prior_right_factor):
    mixed_update = momentum + gradient.astype(jnp.float32)
    partial_value = jnp.einsum(
        "aph,aht->apt", mixed_update, prior_right_factor, precision=lax.Precision.HIGHEST
    )
    left_full = lax.psum(partial_value, ("tensor", "dp"))

    def summer(operand):
        return lax.psum(operand, "shard")

    column_basis = cholesky_pass(cholesky_pass(left_full, summer), summer)
    right_portion = jnp.einsum(
        "wvp,wvc->wpc", mixed_update, column_basis, precision=lax.Precision.HIGHEST
    )
    fresh_right_factor = lax.psum(right_portion, "shard")
    momentum_next = mixed_update - (1.0 - decay_rate) * jnp.einsum(
        "fwd,fad->fwa", column_basis, fresh_right_factor, precision=lax.Precision.HIGHEST
    )
    squares = lax.psum(jnp.sum(fresh_right_factor * fresh_right_factor, axis=1), ("tensor", "dp"))
    scales = jnp.sqrt(squares / N + epsilon)
    following_right_factor = fresh_right_factor / scales[:, None, :]
    direction = jnp.sqrt(M / R) * jnp.einsum(
        "fwd,fad->fwa", column_basis, following_right_factor, precision=lax.Precision.HIGHEST
    )
    return (momentum_next, following_right_factor, direction.astype(jnp.bfloat16))


def solution(mesh):
    return jax.shard_map(
        shards,
        mesh=mesh,
        in_specs=(
            P(None, "shard", ("tensor", "dp")),
            P(None, "shard", ("tensor", "dp")),
            P(None, ("tensor", "dp"), None),
        ),
        out_specs=(
            P(None, "shard", ("tensor", "dp")),
            P(None, ("tensor", "dp"), None),
            P(None, "shard", ("tensor", "dp")),
        ),
        check_vma=False,
    )
```

profile of v0, /device:TPU:0, one launch (start us, length us, event | category | flops | bytes accessed | tf_op | source)
XLA Modules:
  0.0 303.4 jit_solution(12803602012103822525)
XLA Ops:
  7.2 0.0 copy-start
  7.2 0.0 all-reduce.5.cloned.1.call-start
  7.2 1.0 copy-done
  8.2 10.7 %fusion.5 = f32[1,2048,128]{2,1,0:T(8,128)} fusion(f32[1,2048,1024]{2,1,0:T(8,128)} %param.7, bf16[1,2048,1024]{2,1,0:T(8,128)(2,1)} %param.6, f32[1,1024,128]{2,1,0:T(8,128)S(1)} %copy-done), kind=kOutput, calls=%fused_computation.8 | convolution fusion | flops 3225419776 | bytes 14155776 | tf_op jit(solution)/shard_map/aph,aht->apt/dot_general | solution.py:27
  19.0 0.0 all-reduce.5.cloned.1.call-update
  19.0 0.0 all-reduce.7.cloned.1.call-start
  19.0 59.5 %all-reduce.5.cloned.1.call-done = f32[1,2048,128]{2,1,0:T(8,128)} async-done(((f32[1,2048,128]{2,1,0:T(8,128)}), f32[1,2048,128]{2,1,0:T(8,128)}) %all-reduce.5.cloned.1.call-update) | async-done | bytes 1048592 | tf_op jit(solution)/shard_map/psum | solution.py:30
  78.6 4.0 %convolution_bitcast_fusion.3 = f32[1,128,128]{1,2,0:T(8,128)} fusion(f32[1,2048,128]{2,1,0:T(8,128)} %all-reduce.5.cloned.1.call-done), kind=kOutput, calls=%fused_computation.13 | convolution fusion | flops 402653184 | bytes 1114112 | tf_op jit(solution)/shard_map/ktp,ktv->kpv/dot_general | solution.py:15
  82.5 0.0 all-reduce.7.cloned.1.call-update
  82.6 0.2 all-reduce.9.cloned.1.call-start
  82.8 33.5 %all-reduce.7.cloned.1.call-done = f32[1,128,128]{1,2,0:T(8,128)} async-done(((f32[1,128,128]{1,2,0:T(8,128)}), f32[1,128,128]{1,2,0:T(8,128)}) %all-reduce.7.cloned.1.call-update) | async-done | bytes 65552 | tf_op jit(solution)/shard_map/psum | solution.py:33
  116.3 0.9 copy.7
  117.2 0.9 fusion.21
  118.1 11.7 %custom-call.8 = f32[1,128,128]{2,1,0:T(8,128)S(1)} custom-call(f32[1,128,128]{2,1,0:T(8,128)S(1)} %fusion.21), custom_call_target="Cholesky" | custom-call | tf_op jit(solution)/shard_map/jit(cholesky)/cholesky | solution.py:19
  129.8 0.6 compare_reduce_fusion.1
  130.4 0.7 fusion.16
  131.1 9.8 %custom-call.9 = f32[1,1,128,128]{2,3,1,0:T(8,128)S(1)} custom-call(f32[1,1,128,128]{3,2,1,0:T(8,128)S(1)} %fusion.16), custom_call_target="InvertDiagBlocksLowerTriangular" | custom-call | tf_op jit(solution)/shard_map/triangular_solve/custom-call.0 | solution.py:20
  140.9 2.3 convolution_bitcast_fusion.1
  143.2 1.6 convolution_bitcast_fusion.2
  144.8 0.0 all-reduce.9.cloned.1.call-update
  144.9 0.3 all-reduce.11.cloned.1.call-start
  145.1 33.9 %all-reduce.9.cloned.1.call-done = f32[1,128,128]{1,2,0:T(8,128)} async-done(((f32[1,128,128]{1,2,0:T(8,128)}), f32[1,128,128]{1,2,0:T(8,128)}) %all-reduce.9.cloned.1.call-update) | async-done | bytes 65552 | tf_op jit(solution)/shard_map/psum | solution.py:33
  179.0 0.9 copy.9
  179.9 0.9 fusion.19
  180.8 11.7 %custom-call.10 = f32[1,128,128]{2,1,0:T(8,128)S(1)} custom-call(f32[1,128,128]{2,1,0:T(8,128)S(1)} %fusion.19), custom_call_target="Cholesky" | custom-call | tf_op jit(solution)/shard_map/jit(cholesky)/cholesky | solution.py:19
  192.5 0.6 compare_reduce_fusion
  193.2 0.7 fusion.17
  193.8 9.8 %custom-call.11 = f32[1,1,128,128]{2,3,1,0:T(8,128)S(1)} custom-call(f32[1,1,128,128]{3,2,1,0:T(8,128)S(1)} %fusion.17), custom_call_target="InvertDiagBlocksLowerTriangular" | custom-call | tf_op jit(solution)/shard_map/triangular_solve/custom-call.0 | solution.py:20
  203.7 1.1 convolution_bitcast_fusion
  204.7 17.3 %fusion.8 = f32[1,1024,128]{2,1,0:T(8,128)} fusion(f32[2048,128]{0,1:T(8,128)S(1)} %convolution_bitcast_fusion, f32[1,2048,1024]{2,1,0:T(8,128)} %param.7, bf16[1,2048,1024]{2,1,0:T(8,128)(2,1)} %param.6), kind=kOutput, calls=%fused_computation.11 | convolution fusion | flops 3225419776 | bytes 14155776 | tf_op jit(solution)/shard_map/wvp,wvc->wpc/dot_general | solution.py:36
  222.0 0.0 all-reduce.11.cloned.1.call-update
  222.0 38.4 %all-reduce.11.cloned.1.call-done = f32[1,1024,128]{2,1,0:T(8,128)} async-done(((f32[1,1024,128]{2,1,0:T(8,128)}), f32[1,1024,128]{2,1,0:T(8,128)}) %all-reduce.11.cloned.1.call-update) | async-done | bytes 524304 | tf_op jit(solution)/shard_map/psum | solution.py:39
  260.4 1.2 multiply_reduce_fusion
  261.6 13.4 %psum.39 = f32[1,128]{1,0:T(1,128)S(1)} all-reduce(f32[1,128]{1,0:T(1,128)S(1)} %bitcast.76), channel_id=1, replica_groups=mesh['shard'=4,'tensor'=4,'dp'=2] {'tensor','dp'}, use_global_device_ids=true, to_apply=%region_7.10 | all-reduce | flops 128 | bytes 1024 | tf_op jit(solution)/shard_map/psum | solution.py:43
  275.0 0.0 copy-start.1
  275.0 1.2 broadcast_divide_fusion
  276.2 0.0 copy-start.2
  276.2 8.4 %fusion.4 = bf16[1,2048,1024]{2,1,0:T(8,128)(2,1)} fusion(f32[2048,128]{0,1:T(8,128)S(1)} %convolution_bitcast_fusion, f32[1,1024,128]{2,1,0:T(8,128)S(1)} %broadcast_divide_fusion), kind=kOutput, calls=%fused_computation.7 | convolution fusion | flops 3225419776 | bytes 5767168 | tf_op jit(solution)/shard_map/fwd,fad->fwa/dot_general | solution.py:46
  284.6 0.0 copy-done.1
  284.6 12.2 %bitcast_subtract_fusion = f32[1,2048,1024]{2,1,0:T(8,128)} fusion(f32[2048,128]{0,1:T(8,128)S(1)} %convolution_bitcast_fusion, f32[1,2048,1024]{2,1,0:T(8,128)} %param.7, bf16[1,2048,1024]{2,1,0:T(8,128)(2,1)S(1)} %copy-done.1, f32[1,1024,128]{2,1,0:T(8,128)} %all-reduce.11.cloned.1.call-done), kind=kOutput, calls=%fused_computation | convolution fusion | flops 3229614080 | bytes 22544384 | tf_op jit(solution)/shard_map/fwd,fad->fwa/dot_general | solution.py:40
  296.8 0.0 copy-done.2
  (3 shorter events, 0.1 us)
Async XLA Ops:
  7.2 1.0 copy-start
  7.2 71.4 %all-reduce.5.cloned.1.call-start = ((), (), s32[]{:S(2)}) async-start(), calls=%async_computation | async-start | bytes 2097152 | tf_op jit(solution)/shard_map/psum | solution.py:30
  19.0 97.3 %all-reduce.7.cloned.1.call-start = ((), (), s32[]{:S(2)}) async-start(), calls=%async_computation.1 | async-start | bytes 131072 | tf_op jit(solution)/shard_map/psum | solution.py:33
  82.6 96.4 %all-reduce.9.cloned.1.call-start = ((), (), s32[]{:S(2)}) async-start(), calls=%async_computation.2 | async-start | bytes 131072 | tf_op jit(solution)/shard_map/psum | solution.py:33
  144.9 115.5 %all-reduce.11.cloned.1.call-start = ((), (), s32[]{:S(2)}) async-start(), calls=%async_computation.3 | async-start | bytes 1048576 | tf_op jit(solution)/shard_map/psum | solution.py:39
  275.0 9.7 %copy-start.1 = (bf16[1,2048,1024]{2,1,0:T(8,128)(2,1)S(1)}, bf16[1,2048,1024]{2,1,0:T(8,128)(2,1)}, u32[]{:S(2)}) copy-start(bf16[1,2048,1024]{2,1,0:T(8,128)(2,1)} %param.6) | copy-start | bytes 12582916
  276.2 20.6 %copy-start.2 = (f32[1,1024,128]{2,1,0:T(8,128)}, f32[1,1024,128]{2,1,0:T(8,128)S(1)}, u32[]{:S(2)}) copy-start(f32[1,1024,128]{2,1,0:T(8,128)S(1)} %broadcast_divide_fusion) | copy-start | bytes 1572868
Sparse Core Ops, SparseCore 0:
  19.1 59.4 all-reduce.4
  82.7 33.5 all-reduce.6
  145.0 33.9 all-reduce.8
  222.1 38.1 all-reduce.10
where the time goes:
time: 304 us; the launch traced here: 303 us
  waiting for transfers between devices  165 us (54%)
  matrix products  57.6 us (19%)
  other arithmetic  49.9 us (16%)
  between operations  13.9 us (5%)
  blocking collectives  13.4 us (4%)
    psum x2, waiting for transfers between devices, summer(): return lax.psum(operand, 'shard')  67.3 us
    psum x1, waiting for transfers between devices, shards(): left_full = lax.psum(partial_value, ('tensor', 'dp'))  59.5 us
    psum x1, waiting for transfers between devices, shards(): fresh_right_factor = lax.psum(right_portion, 'shard')  38.4 us
    another operation x6, other arithmetic, cholesky_pass(): factor_lower = jnp.linalg.cholesky(gram_matrix)  24.8 us
    another operation x4, other arithmetic, cholesky_pass(): lax.linalg.triangular_solve(factor_lower, row_segment_block, left_side=Fa...  20.9 us
    dot_general x1, matrix products, shards(): jnp.einsum('wvp,wvc->wpc', mixed_update, column_basis, precision=lax.Prec...  17.3 us
    psum x1, blocking collectives, shards(): lax.psum(jnp.sum(fresh_right_factor * fresh_right_factor, axis=1), ('tens...  13.4 us
    dot_general x1, matrix products, shards(): jnp.einsum('fwd,fad->fwa', column_basis, fresh_right_factor, precision=la...  12.2 us
  transfers between devices with their start and end apart: 4, of which 4 were waited for; matrix products, arithmetic and copies ran while one was open for 0% of the time, Pallas kernels for 0%

commit v1 on v0

--- a/solution.py
+++ b/solution.py
@@ -27,7 +27,7 @@
     partial_value = jnp.einsum(
         "aph,aht->apt", mixed_update, prior_right_factor, precision=lax.Precision.HIGHEST
     )
-    left_full = lax.psum(partial_value, ("tensor", "dp"))
+    left_full = lax.psum(lax.psum(partial_value, "dp"), "tensor")
 
     def summer(operand):
         return lax.psum(operand, "shard")

time: 304 us -> 327 us (1.076)
  waiting for transfers between devices: 165 us -> 189 us
    psum x1 -> x2, waiting for transfers between devices: 59.5 us -> 81.5 us  [shards(): left_full = lax.psum(lax.psum(partial_value, 'dp'), 'tensor')]
  transfers between devices with their start and end apart: 4 -> 5, of which waited for: 4 -> 5; matrix products, arithmetic and copies ran while one was open for 0% -> 0% of each run, Pallas kernels for 0% -> 0%
where the time goes in v1:
time: 327 us
  waiting for transfers between devices  189 us (58%)
  matrix products  57.6 us (18%)
  other arithmetic  49.9 us (15%)
  between operations  13.9 us (4%)
  blocking collectives  13.4 us (4%)
    psum x2, waiting for transfers between devices, shards(): left_full = lax.psum(lax.psum(partial_value, 'dp'), 'tensor')  81.5 us
    psum x2, waiting for transfers between devices, summer(): return lax.psum(operand, 'shard')  68.6 us
    psum x1, waiting for transfers between devices, shards(): fresh_right_factor = lax.psum(right_portion, 'shard')  38.5 us
    another operation x6, other arithmetic, cholesky_pass(): factor_lower = jnp.linalg.cholesky(gram_matrix)  24.8 us
    another operation x4, other arithmetic, cholesky_pass(): lax.linalg.triangular_solve(factor_lower, row_segment_block, left_side=Fa...  20.9 us
    dot_general x1, matrix products, shards(): jnp.einsum('wvp,wvc->wpc', mixed_update, column_basis, precision=lax.Prec...  17.3 us
    psum x1, blocking collectives, shards(): lax.psum(jnp.sum(fresh_right_factor * fresh_right_factor, axis=1), ('tens...  13.4 us
    dot_general x1, matrix products, shards(): jnp.einsum('fwd,fad->fwa', column_basis, fresh_right_factor, precision=la...  12.2 us
  transfers between devices with their start and end apart: 5, of which 5 were waited for; matrix products, arithmetic and copies ran while one was open for 0% of the time, Pallas kernels for 0%

profile of v1, /device:TPU:0, one launch (start us, length us, event | category | flops | bytes accessed | tf_op | source)
XLA Modules:
  0.0 326.8 jit_solution(13414634869031526581)
XLA Ops:
  7.2 0.0 copy-start
  7.2 0.0 all-reduce.6.cloned.1.call-start
  7.2 1.0 copy-done
  8.2 10.7 %fusion.5 = f32[1,2048,128]{2,1,0:T(8,128)} fusion(f32[1,2048,1024]{2,1,0:T(8,128)} %param.7, bf16[1,2048,1024]{2,1,0:T(8,128)(2,1)} %param.6, f32[1,1024,128]{2,1,0:T(8,128)S(1)} %copy-done), kind=kOutput, calls=%fused_computation.8 | convolution fusion | flops 3225419776 | bytes 14155776 | tf_op jit(solution)/shard_map/aph,aht->apt/dot_general | solution.py:27
  19.0 0.0 all-reduce.6.cloned.1.call-update
  19.0 0.0 all-reduce.8.cloned.1.call-start
  19.0 42.9 %all-reduce.6.cloned.1.call-done = f32[1,2048,128]{2,1,0:T(8,128)} async-done(((f32[1,2048,128]{2,1,0:T(8,128)}), f32[1,2048,128]{2,1,0:T(8,128)}) %all-reduce.6.cloned.1.call-update) | async-done | bytes 1048592 | tf_op jit(solution)/shard_map/psum | solution.py:30
  62.0 0.0 all-reduce.8.cloned.1.call-update
  62.0 0.0 all-reduce.10.cloned.1.call-start
  62.0 38.6 %all-reduce.8.cloned.1.call-done = f32[1,2048,128]{2,1,0:T(8,128)} async-done(((f32[1,2048,128]{2,1,0:T(8,128)}), f32[1,2048,128]{2,1,0:T(8,128)}) %all-reduce.8.cloned.1.call-update) | async-done | bytes 1048592 | tf_op jit(solution)/shard_map/psum | solution.py:30
  100.6 4.0 %convolution_bitcast_fusion.3 = f32[1,128,128]{1,2,0:T(8,128)} fusion(f32[1,2048,128]{2,1,0:T(8,128)} %all-reduce.8.cloned.1.call-done), kind=kOutput, calls=%fused_computation.13 | convolution fusion | flops 402653184 | bytes 1114112 | tf_op jit(solution)/shard_map/ktp,ktv->kpv/dot_general | solution.py:15
  104.6 0.0 all-reduce.10.cloned.1.call-update
  104.7 0.2 all-reduce.12.cloned.1.call-start
  104.9 34.7 %all-reduce.10.cloned.1.call-done = f32[1,128,128]{1,2,0:T(8,128)} async-done(((f32[1,128,128]{1,2,0:T(8,128)}), f32[1,128,128]{1,2,0:T(8,128)}) %all-reduce.10.cloned.1.call-update) | async-done | bytes 65552 | tf_op jit(solution)/shard_map/psum | solution.py:33
  139.6 0.9 copy.7
  140.5 0.9 fusion.21
  141.4 11.7 %custom-call.8 = f32[1,128,128]{2,1,0:T(8,128)S(1)} custom-call(f32[1,128,128]{2,1,0:T(8,128)S(1)} %fusion.21), custom_call_target="Cholesky" | custom-call | tf_op jit(solution)/shard_map/jit(cholesky)/cholesky | solution.py:19
  153.1 0.6 compare_reduce_fusion.1
  153.8 0.7 fusion.16
  154.4 9.8 %custom-call.9 = f32[1,1,128,128]{2,3,1,0:T(8,128)S(1)} custom-call(f32[1,1,128,128]{3,2,1,0:T(8,128)S(1)} %fusion.16), custom_call_target="InvertDiagBlocksLowerTriangular" | custom-call | tf_op jit(solution)/shard_map/triangular_solve/custom-call.0 | solution.py:20
  164.2 2.3 convolution_bitcast_fusion.1
  166.5 1.6 convolution_bitcast_fusion.2
  168.1 0.0 all-reduce.12.cloned.1.call-update
  168.2 0.3 all-reduce.14.cloned.1.call-start
  168.4 33.9 %all-reduce.12.cloned.1.call-done = f32[1,128,128]{1,2,0:T(8,128)} async-done(((f32[1,128,128]{1,2,0:T(8,128)}), f32[1,128,128]{1,2,0:T(8,128)}) %all-reduce.12.cloned.1.call-update) | async-done | bytes 65552 | tf_op jit(solution)/shard_map/psum | solution.py:33
  202.3 0.9 copy.9
  203.2 0.9 fusion.19
  204.1 11.7 %custom-call.10 = f32[1,128,128]{2,1,0:T(8,128)S(1)} custom-call(f32[1,128,128]{2,1,0:T(8,128)S(1)} %fusion.19), custom_call_target="Cholesky" | custom-call | tf_op jit(solution)/shard_map/jit(cholesky)/cholesky | solution.py:19
  215.8 0.6 compare_reduce_fusion
  216.5 0.7 fusion.17
  217.2 9.8 %custom-call.11 = f32[1,1,128,128]{2,3,1,0:T(8,128)S(1)} custom-call(f32[1,1,128,128]{3,2,1,0:T(8,128)S(1)} %fusion.17), custom_call_target="InvertDiagBlocksLowerTriangular" | custom-call | tf_op jit(solution)/shard_map/triangular_solve/custom-call.0 | solution.py:20
  227.0 1.1 convolution_bitcast_fusion
  228.0 17.3 %fusion.8 = f32[1,1024,128]{2,1,0:T(8,128)} fusion(f32[2048,128]{0,1:T(8,128)S(1)} %convolution_bitcast_fusion, f32[1,2048,1024]{2,1,0:T(8,128)} %param.7, bf16[1,2048,1024]{2,1,0:T(8,128)(2,1)} %param.6), kind=kOutput, calls=%fused_computation.11 | convolution fusion | flops 3225419776 | bytes 14155776 | tf_op jit(solution)/shard_map/wvp,wvc->wpc/dot_general | solution.py:36
  245.3 0.0 all-reduce.14.cloned.1.call-update
  245.3 38.5 %all-reduce.14.cloned.1.call-done = f32[1,1024,128]{2,1,0:T(8,128)} async-done(((f32[1,1024,128]{2,1,0:T(8,128)}), f32[1,1024,128]{2,1,0:T(8,128)}) %all-reduce.14.cloned.1.call-update) | async-done | bytes 524304 | tf_op jit(solution)/shard_map/psum | solution.py:39
  283.8 1.2 multiply_reduce_fusion
  285.0 13.4 %psum.47 = f32[1,128]{1,0:T(1,128)S(1)} all-reduce(f32[1,128]{1,0:T(1,128)S(1)} %bitcast.76), channel_id=1, replica_groups=mesh['shard'=4,'tensor'=4,'dp'=2] {'tensor','dp'}, use_global_device_ids=true, to_apply=%region_8.11 | all-reduce | flops 128 | bytes 1024 | tf_op jit(solution)/shard_map/psum | solution.py:43
  298.4 0.0 copy-start.1
  298.4 1.2 broadcast_divide_fusion
  299.7 0.0 copy-start.2
  299.7 8.4 %fusion.4 = bf16[1,2048,1024]{2,1,0:T(8,128)(2,1)} fusion(f32[2048,128]{0,1:T(8,128)S(1)} %convolution_bitcast_fusion, f32[1,1024,128]{2,1,0:T(8,128)S(1)} %broadcast_divide_fusion), kind=kOutput, calls=%fused_computation.7 | convolution fusion | flops 3225419776 | bytes 5767168 | tf_op jit(solution)/shard_map/fwd,fad->fwa/dot_general | solution.py:46
  308.1 0.0 copy-done.1
  308.1 12.2 %bitcast_subtract_fusion = f32[1,2048,1024]{2,1,0:T(8,128)} fusion(f32[2048,128]{0,1:T(8,128)S(1)} %convolution_bitcast_fusion, f32[1,2048,1024]{2,1,0:T(8,128)} %param.7, bf16[1,2048,1024]{2,1,0:T(8,128)(2,1)S(1)} %copy-done.1, f32[1,1024,128]{2,1,0:T(8,128)} %all-reduce.14.cloned.1.call-done), kind=kOutput, calls=%fused_computation | convolution fusion | flops 3229614080 | bytes 22544384 | tf_op jit(solution)/shard_map/fwd,fad->fwa/dot_general | solution.py:40
  320.3 0.0 copy-done.2
  (3 shorter events, 0.1 us)
Async XLA Ops:
  7.2 1.0 copy-start
  7.2 54.8 %all-reduce.6.cloned.1.call-start = ((), (), s32[]{:S(2)}) async-start(), calls=%async_computation | async-start | bytes 2097152 | tf_op jit(solution)/shard_map/psum | solution.py:30
  19.0 81.6 %all-reduce.8.cloned.1.call-start = ((), (), s32[]{:S(2)}) async-start(), calls=%async_computation.1 | async-start | bytes 2097152 | tf_op jit(solution)/shard_map/psum | solution.py:30
  62.0 77.6 %all-reduce.10.cloned.1.call-start = ((), (), s32[]{:S(2)}) async-start(), calls=%async_computation.2 | async-start | bytes 131072 | tf_op jit(solution)/shard_map/psum | solution.py:33
  104.7 97.7 %all-reduce.12.cloned.1.call-start = ((), (), s32[]{:S(2)}) async-start(), calls=%async_computation.3 | async-start | bytes 131072 | tf_op jit(solution)/shard_map/psum | solution.py:33
  168.2 115.7 %all-reduce.14.cloned.1.call-start = ((), (), s32[]{:S(2)}) async-start(), calls=%async_computation.4 | async-start | bytes 1048576 | tf_op jit(solution)/shard_map/psum | solution.py:39
  298.4 9.7 %copy-start.1 = (bf16[1,2048,1024]{2,1,0:T(8,128)(2,1)S(1)}, bf16[1,2048,1024]{2,1,0:T(8,128)(2,1)}, u32[]{:S(2)}) copy-start(bf16[1,2048,1024]{2,1,0:T(8,128)(2,1)} %param.6) | copy-start | bytes 12582916
  299.7 20.6 %copy-start.2 = (f32[1,1024,128]{2,1,0:T(8,128)}, f32[1,1024,128]{2,1,0:T(8,128)S(1)}, u32[]{:S(2)}) copy-start(f32[1,1024,128]{2,1,0:T(8,128)S(1)} %broadcast_divide_fusion) | copy-start | bytes 1572868
Sparse Core Ops, SparseCore 0:
  19.1 42.8 all-reduce.5
  64.3 36.2 all-reduce.7
  104.8 34.7 all-reduce.9
  168.3 33.9 all-reduce.11
  245.4 38.3 all-reduce.13
